TPU v7x, 32 devices: a whole 2x2x4 slice. The times are simulated.
32 devices in a mesh: batch: 2 (over y), freq: 8 (over z, x), elem: 2 (over core).
Axes of the slice: x: 2, y: 2, z: 4, core: 2. Of those that a mesh axis runs over, the one named last changes fastest.
Arguments:
- flaw_cells: int32 [512], P('batch'), parts along dimension 0, may hold values from 0 to 255, each once
- flaw_blocks: int32 [16], P('batch'), parts along dimension 0, may hold values from 0 to 7, each once
- element_channel: int32 [256], P('elem'), may hold values from 0 to 255, each once
- focal_delay: float32 [256, 256], replicated, may hold values from 0 to 64
- beam_field: bfloat16 [128, 2, 256, 256], P('freq', None, 'elem'), may hold values from -0.125 to 0.125
- flaw_size: float32 [4, 128], P('batch'), parts along dimension 0, may hold values from 0.5 to 4
- flaw_slope: float32 [4, 128], P('batch'), parts along dimension 0, may hold values from 0.2 to 1
- noise_level: float32 [4, 128], P(('batch', 'elem'), 'freq'), parts along dimension 0, may hold values from 0.5 to 5
Outputs:
- flaw_peak: float32 [4, 128], P(('batch', 'elem'), 'freq'), parts along dimension 0
- detection: float32 [4, 128], P(('batch', 'elem'), 'freq'), parts along dimension 0
There are 2 independent parts, one for each index of `batch`. A program takes and returns all parts, laid end to end along the dimension named above; an argument that names none is the same for every part. Nothing has to cross between parts.
Inputs may be any that keep to these rules, and one draw needn't show every extreme that they name: `flaw_cells`: every site holds exactly one flaw. `flaw_blocks`: every scan block belongs to exactly one flaw group. `element_channel`: every channel drives exactly one element.
All inputs are finite; a program needn't handle non-finite values.
Results may differ from a plain program's by a relative error of at most 0.0011.
Values may be sent and summed in bfloat16 or wider, within the bound.
A program may use at most 64 MiB of HBM per device.

v0:
```python
import math
import jax
import jax.numpy as jnp
from jax import lax
from jax.sharding import PartitionSpec as P

W_DEV = 16
FG = 128
NB = 4
SB = 32
T_CAP = 1024
EDGE = 0.6
STEEP = 3.0
EPS = 1e-05


def kirchhoff(angular, flaw_size, flaw_slope):
    angles = angular[None, :, None] * (2.0 * flaw_size * flaw_slope)[:, None, :]
    real_part = flaw_size[:, None, :] * (1.0 + EDGE) * jnp.cos(angles)
    imag_part = flaw_size[:, None, :] * (EDGE - 1.0) * jnp.sin(angles)
    return (real_part, imag_part)


def focal_law(angular, delays):
    phases = angular[:, None, None, None] * delays[None]
    return jnp.concatenate([jnp.cos(phases), -jnp.sin(phases)], axis=-1).astype(jnp.bfloat16)


def field_matrix(fields):
    real_part = fields[:, 0]
    imag_part = fields[:, 1]
    upper_rows = jnp.concatenate([real_part, imag_part], axis=-1)
    lower_rows = jnp.concatenate([-imag_part, real_part], axis=-1)
    return jnp.concatenate([upper_rows, lower_rows], axis=1)


def combine(product, k_real, k_imag):
    columns = k_real.shape[-1]
    real_part = product[..., :columns]
    imag_part = product[..., columns:]
    scale_real = k_real[:, :, None, :]
    scale_imag = k_imag[:, :, None, :]
    return jnp.stack(
        [
            scale_real * real_part - scale_imag * imag_part,
            scale_real * imag_part + scale_imag * real_part,
        ],
        axis=2,
    )


def envelope_peak(spectra, row_count):
    groups, freq_total, planes, columns = spectra.shape
    sample_count = min(T_CAP, 2 * freq_total)
    time_block = min(128, sample_count)
    freq_index = jnp.arange(freq_total, dtype=jnp.int32)
    scaling = 1.0 / math.sqrt(freq_total)

    def advance(step_index, running):
        sample_times = step_index * time_block + jnp.arange(time_block, dtype=jnp.int32)
        phase_steps = freq_index[:, None] * sample_times[None, :] % (2 * freq_total)
        angles = phase_steps.astype(jnp.float32) * (math.pi / freq_total)
        cosine = jnp.cos(angles)
        sine_part = jnp.sin(angles)
        twiddle = jnp.stack(
            [jnp.stack([cosine, sine_part], axis=1), jnp.stack([-sine_part, cosine], axis=1)],
            axis=1,
        )
        twiddle_high = lax.optimization_barrier(twiddle.astype(jnp.bfloat16))
        twiddle_low = (twiddle - twiddle_high.astype(jnp.float32)).astype(jnp.bfloat16)
        signal = jnp.einsum(
            "gwcx,wckt->gkxt", spectra, twiddle_high, preferred_element_type=jnp.float32
        )
        signal = signal + jnp.einsum(
            "gwcx,wckt->gkxt", spectra, twiddle_low, preferred_element_type=jnp.float32
        )
        signal = signal * scaling
        magnitude = jnp.sqrt(signal[:, 0] * signal[:, 0] + signal[:, 1] * signal[:, 1])
        magnitude = magnitude.reshape(groups, row_count, columns // row_count, time_block)
        return jnp.maximum(running, jnp.max(magnitude, axis=(1, 3)))

    initial = jnp.zeros((groups, columns // row_count), jnp.float32)
    return lax.fori_loop(0, sample_count // time_block, advance, initial)


def regroup_peaks(moved):
    groups, freq_total, planes, row_count, flaw_count = moved.shape
    return envelope_peak(
        moved.reshape(groups, freq_total, planes, row_count * flaw_count), row_count
    )


def body(
    flaw_cells,
    flaw_blocks,
    element_channel,
    focal_delay,
    beam_field,
    flaw_size,
    flaw_slope,
    noise_level,
):
    freq_count = lax.axis_size("freq")
    freq_total = W_DEV * freq_count
    group_total = flaw_size.shape[0]
    row_total = NB * SB
    first_freq = lax.axis_index("freq") * W_DEV
    angular = (first_freq + jnp.arange(W_DEV, dtype=jnp.int32)).astype(jnp.float32) * (
        math.pi / freq_total
    )
    scan_rows = (
        flaw_blocks.reshape(group_total, NB)[:, :, None] * SB
        + jnp.arange(SB, dtype=jnp.int32)[None, None, :]
    ).reshape(group_total, row_total)
    delays = jnp.moveaxis(
        jnp.take(jnp.take(focal_delay, element_channel, axis=0), scan_rows, axis=1), 0, 2
    )
    fields = jnp.take(beam_field, flaw_cells, axis=3).reshape(
        W_DEV, 2, element_channel.shape[0], group_total, FG
    )
    k_real, k_imag = kirchhoff(angular, flaw_size, flaw_slope)
    focal_terms = focal_law(angular, delays)
    field_terms = field_matrix(fields)
    product = jnp.einsum(
        "wgre,wegf->gwrf", focal_terms, field_terms, preferred_element_type=jnp.float32
    )
    partial_value = combine(product, k_real, k_imag).astype(jnp.bfloat16)
    rounded_term = lax.optimization_barrier(partial_value).astype(jnp.float32)
    summed = lax.psum_scatter(
        rounded_term.astype(jnp.bfloat16), "elem", scatter_dimension=0, tiled=True
    )
    partial_peak = regroup_peaks(
        lax.all_to_all(summed, "freq", split_axis=3, concat_axis=1, tiled=True)
    )
    whole_peak = lax.pmax(partial_peak, "freq")
    columns = FG // freq_count
    flaw_peak = lax.dynamic_slice_in_dim(whole_peak, lax.axis_index("freq") * columns, columns, 1)
    detection = jax.nn.sigmoid(STEEP * (jnp.log(flaw_peak + EPS) - jnp.log(noise_level)))
    return (flaw_peak, detection)


def solution(mesh):
    in_specs = (
        P("batch"),
        P("batch"),
        P("elem"),
        P(),
        P("freq", None, "elem", None),
        P("batch", None),
        P("batch", None),
        P(("batch", "elem"), "freq"),
    )
    out_specs = (P(("batch", "elem"), "freq"), P(("batch", "elem"), "freq"))
    return jax.shard_map(body, mesh=mesh, in_specs=in_specs, out_specs=out_specs, check_vma=False)
```

profile of v0, /device:TPU:0, one launch (start us, length us, event | category | flops | bytes accessed | tf_op | source)
XLA Modules:
  0.0 130.7 jit_solution(10028995258592045228)
XLA Ops:
  7.2 0.0 copy-start
  7.2 0.0 all-reduce.3.cloned.1.call-start
  7.2 0.7 compare_select_fusion.3
  7.9 1.2 compare_and_fusion
  9.1 0.7 broadcast_multiply_fusion.2
  9.7 0.1 mul.298
  9.8 0.1 add.209
  9.9 0.1 add.219
  10.0 0.1 add.210
  10.1 0.7 compare_select_fusion
  10.8 0.7 and_bitcast_fusion
  11.4 3.5 %copy.28 = bf16[16,2,128,256]{2,0,3,1:T(8,128)(2,1)S(1)} copy(bf16[16,2,128,256]{3,2,1,0:T(8,128)(2,1)} %param.14) | data formatting | bytes 4194304 | tf_op args[4]
  14.9 2.3 %gather_fusion.2 = bf16[256,16,2,128]{3,1,2,0:T(8,128)(2,1)} fusion(bf16[16,2,128,256]{2,0,3,1:T(8,128)(2,1)S(1)} %copy.28, s32[1024]{0:T(1024)S(1)} %pad_clamp_fusion), kind=kCustom, calls=%fused_computation.2 | custom fusion | bytes 4195328 | tf_op jit(solution)/shard_map/jit(_take)/gather | solution.py:118
  17.2 3.5 %copy.30 = bf16[16,2,128,2,128]{4,2,0,3,1:T(8,128)(2,1)S(1)} copy(bf16[16,2,128,2,128]{2,0,1,4,3:T(8,128)(2,1)} %bitcast.85) | data formatting | bytes 4194304 | tf_op jit(solution)/shard_map/jit(_take)/gather | solution.py:118
  20.7 0.2 broadcast_select_fusion.1
  20.9 0.1 slice_bitcast_fusion
  21.0 0.1 fusion.42
  21.2 0.1 add.212
  21.3 0.0 copy-done
  21.3 0.8 gather_fusion
  22.1 1.4 %broadcast_select_fusion.3 = f32[128,256]{1,0:T(8,128)} fusion(f32[128,256]{1,0:T(8,128)S(1)} %gather_fusion, pred[128]{0:T(512)(128)(4,1)} %compare_and_fusion), kind=kLoop, calls=%fused_computation.64 | loop fusion | flops 32768 | bytes 262272 | tf_op jit(solution)/shard_map/jit(_take)/select_n | solution.py:116
  23.5 1.0 copy.27
  24.5 0.5 compare_and_fusion.1
  25.0 1.3 %gather_fusion.1 = f32[256,128]{1,0:T(8,128)} fusion(f32[128,256]{0,1:T(8,128)S(1)} %copy.27, s32[1024]{0:T(1024)S(1)} %pad_clamp_fusion.1), kind=kCustom, calls=%fused_computation.1 | custom fusion | bytes 263168 | tf_op jit(solution)/shard_map/jit(_take)/gather | solution.py:116
  26.3 1.0 broadcast_select_fusion.2
  27.3 7.8 %fusion.30 = (bf16[16,2,128,128]{3,2,0,1:T(8,128)(2,1)S(1)}, bf16[16,2,128,128]{3,2,0,1:T(8,128)(2,1)S(1)}) fusion(f32[2,128,128]{2,1,0:T(8,128)S(1)} %broadcast_select_fusion.2, f32[16]{0:T(128)S(1)} %convert_multiply_fusion), kind=kLoop, calls=%fused_computation.49 | loop fusion | flops 2097152 | bytes 2228288 | tf_op jit(solution)/shard_map/convert.4
  35.1 0.7 broadcast_multiply_fusion.1
  35.9 0.1 fusion.38
  36.0 1.4 %fusion.22 = f32[2,16,128,256]{3,2,1,0:T(8,128)S(1)} fusion(bf16[16,128,2,128]{3,1,0,2:T(8,128)(2,1)S(1)} %get-tuple-element.144, bf16[16,128,2,128]{3,1,0,2:T(8,128)(2,1)S(1)} %fusion.42, bf16[16,128,2,128]{3,1,0,2:T(8,128)(2,1)S(1)} %get-tuple-element.143, bf16[16,2,128,128]{3,2,0,1:T(8,128)(2,1)S(1)} %get-tuple-element.146, ...), kind=kOutput, calls=%fused_computation.39 | convolution fusion | flops 557842432 | bytes 9437184 | tf_op jit(solution)/shard_map/wgre,wegf->gwrf/dot_general | solution.py:124
  37.4 0.6 fusion.36
  38.1 1.5 %pad_maximum_fusion.1 = bf16[2,16,2,128,128]{4,3,1,0,2:T(8,128)(2,1)} fusion(bf16[2,16,1,128,128]{4,3,1,0,2:T(8,128)(2,1)S(1)} %get-tuple-element.142, bf16[2,16,1,128,128]{4,3,1,0,2:T(8,128)(2,1)S(1)} %get-tuple-element.141), kind=kLoop, calls=%fused_computation.55 | loop fusion | flops 1048576 | bytes 4194304 | tf_op jit(solution)/shard_map/stack | solution.py:43
  39.5 0.0 copy-start.2
  39.5 0.0 all-reduce.3.cloned.1.call-update
  39.6 0.6 copy-done.2
  40.2 0.6 dynamic-slice
  40.8 22.9 %all-reduce.3.cloned.1.call-done = bf16[2,16,2,128,128]{4,3,1,0,2:T(8,128)(2,1)} async-done(((bf16[2,16,2,128,128]{4,3,1,0,2:T(8,128)(2,1)}), bf16[2,16,2,128,128]{4,3,1,0,2:T(8,128)(2,1)}) %all-reduce.3.cloned.1.call-update) | async-done | bytes 2097168
  63.6 1.9 %constant_dynamic-slice_fusion = bf16[1,16,2,128,128]{4,3,1,0,2:T(8,128)(2,1)S(1)} fusion(bf16[2,16,2,128,128]{4,3,1,0,2:T(8,128)(2,1)} %all-reduce.3.cloned.1.call-done, u32[]{:T(128)} %bitcast.34), kind=kLoop, calls=%fused_computation.81 | loop fusion | bytes 2097156
  65.6 1.7 %copy.31 = bf16[1,16,2,128,128]{4,1,0,2,3:T(8,128)(2,1)} copy(bf16[1,16,2,128,128]{4,3,1,0,2:T(8,128)(2,1)S(1)} %constant_dynamic-slice_fusion) | data formatting | bytes 2097152 | tf_op jit(solution)/shard_map/reduce_scatter | solution.py:129
  67.2 5.8 %all-to-all-start = ((bf16[1,16,2,128,128]{4,1,0,2,3:T(8,128)(2,1)}), bf16[1,16,2,128,128]{4,1,0,2,3:T(8,128)(2,1)S(1)}, u32[]{:S(2)}, u32[]{:S(2)}) async-start(bf16[1,16,2,128,128]{4,1,0,2,3:T(8,128)(2,1)} %copy.31), calls=%async_computation | async-start | bytes 2097152 | tf_op jit(solution)/shard_map/all_to_all | solution.py:133
  73.0 26.2 %all-to-all-done = bf16[1,16,2,128,128]{4,1,0,2,3:T(8,128)(2,1)S(1)} async-done(((bf16[1,16,2,128,128]{4,1,0,2,3:T(8,128)(2,1)}), bf16[1,16,2,128,128]{4,1,0,2,3:T(8,128)(2,1)S(1)}, u32[]{:S(2)}, u32[]{:S(2)}) %all-to-all-start) | async-done | bytes 1048608 | tf_op jit(solution)/shard_map/all_to_all | solution.py:133
  99.2 0.4 copy.32
  99.7 0.5 reshape.333
  100.2 0.0 copy-start.1
  100.2 3.5 %while.16 = (s32[]{:T(128)}, f32[1,128]{1,0:T(1,128)S(1)}, bf16[1,128,2,2048]{3,1,2,0:T(8,128)(2,1)S(1)}, s32[]{:T(128)}, s32[]{:T(128)}, /*index=5*/s32[]{:T(128)}) while((s32[]{:T(128)}, f32[1,128]{1,0:T(1,128)S(1)}, bf16[1,128,2,2048]{3,1,2,0:T(8,128)(2,1)S(1)}, s32[]{:T(128)}, s32[]{:T(128)}, /*index=5*/s32[]{:T(128)}) %tuple.58), condition=%wide.region_4.5_spmd.clone, body=%wide.region_1.4_spmd.clone.sunk | while | flops 539607296 | bytes 12078175 | solution.py:83
  100.2 0.3 fusion.55
  100.6 0.4 convolution_bitcast_fusion.3
  101.0 0.5 fusion.57
  101.5 0.4 fusion.58
  102.0 0.3 fusion.55
  102.4 0.4 convolution_bitcast_fusion.3
  102.8 0.5 fusion.57
  103.3 0.4 fusion.58
  103.7 19.5 %pmax.7 = f32[1,128]{1,0:T(1,128)S(1)} all-reduce(f32[1,128]{1,0:T(1,128)S(1)} %get-tuple-element.113), channel_id=1, replica_groups=mesh['batch'=2,'freq'=8,'elem'=2] {'freq'}, use_global_device_ids=true, to_apply=%region_5.6 | all-reduce | flops 128 | bytes 1024 | tf_op jit(solution)/shard_map/pmax | solution.py:135
  123.2 0.0 copy-done.1
  123.2 0.6 add_divide_fusion
  (17 shorter events, 0.2 us)
Async XLA Ops:
  7.2 14.1 %copy-start = (f32[256,256]{1,0:T(8,128)S(1)}, f32[256,256]{1,0:T(8,128)}, u32[]{:S(2)}) copy-start(f32[256,256]{1,0:T(8,128)} %param.13) | copy-start | bytes 786436
  7.2 56.5 %all-reduce.3.cloned.1.call-start = ((), (), s32[]{:S(2)}) async-start(), calls=%async_computation.1 | async-start | bytes 4194304
  39.5 0.7 copy-start.2
  67.2 32.0 %all-to-all-start = ((bf16[1,16,2,128,128]{4,1,0,2,3:T(8,128)(2,1)}), bf16[1,16,2,128,128]{4,1,0,2,3:T(8,128)(2,1)S(1)}, u32[]{:S(2)}, u32[]{:S(2)}) async-start(bf16[1,16,2,128,128]{4,1,0,2,3:T(8,128)(2,1)} %copy.31), calls=%async_computation | async-start | bytes 2097152 | tf_op jit(solution)/shard_map/all_to_all | solution.py:133
  100.2 23.0 %copy-start.1 = (f32[1,16]{1,0:T(1,128)S(1)}, f32[1,16]{1,0:T(1,128)}, u32[]{:S(2)}) copy-start(f32[1,16]{1,0:T(1,128)} %param.17) | copy-start | bytes 196
Sparse Core Ops, SparseCore 0:
  39.7 23.9 all-reduce.2
where the time goes:
time: 131 us
  waiting for transfers between devices  49.1 us (37%)
  other arithmetic  20.2 us (15%)
  blocking collectives  19.5 us (15%)
  local copies, waits for them, and re-layouts  18.6 us (14%)
  between operations  14.2 us (11%)
  starting transfers between devices  5.81 us (4%)
  matrix products  3.2 us (2%)
    all_to_all x1, waiting for transfers between devices, body(): lax.all_to_all(summed, 'freq', split_axis=3, concat_axis=1, tiled=True)  26.2 us
    unnamed x2, waiting for transfers between devices  22.9 us
    pmax x1, blocking collectives, body(): whole_peak = lax.pmax(partial_peak, 'freq')  19.5 us
    another operation x1, other arithmetic  7.81 us
    unnamed x9, local copies, waits for them, and re-layouts  6.63 us
    all_to_all x1, starting transfers between devices, body(): lax.all_to_all(summed, 'freq', split_axis=3, concat_axis=1, tiled=True)  5.78 us
    gather x2, local copies, waits for them, and re-layouts, body(): jnp.take(beam_field, flaw_cells, axis=3)  5.75 us
  transfers between devices with their start and end apart: 2, of which 2 were waited for; matrix products, arithmetic and copies ran while one was open for 0% of the time, Pallas kernels for 0%

commit v1 on v0

--- a/solution.py
+++ b/solution.py
@@ -12,6 +12,28 @@
 EDGE = 0.6
 STEEP = 3.0
 EPS = 1e-05
+
+
+def in_blocks(x, dim, peers):
+    before, after = (x.shape[:dim], x.shape[dim + 1 :])
+    return jnp.moveaxis(x.reshape(*before, peers, -1, *after), dim, 0)
+
+
+def in_order(parts, dim):
+    parts = jnp.moveaxis(parts, 0, dim)
+    shape = parts.shape
+    return parts.reshape(*shape[:dim], shape[dim] * shape[dim + 1], *shape[dim + 2 :])
+
+
+def sent_to_each(array, axis, split_dim, concat_dim):
+    count, here = (lax.axis_size(axis), lax.axis_index(axis))
+    blocks = in_blocks(array, split_dim, count)
+    outs = [blocks[here]]
+    for step in range(1, count):
+        sent = blocks[(here + step) % count]
+        outs.append(lax.ppermute(sent, axis, [(i, (i + step) % count) for i in range(count)]))
+    blocks = jnp.stack(outs)[(here - jnp.arange(count)) % count]
+    return in_order(blocks, concat_dim)
 
 
 def kirchhoff(angular, flaw_size, flaw_slope):
@@ -129,9 +151,7 @@
     summed = lax.psum_scatter(
         rounded_term.astype(jnp.bfloat16), "elem", scatter_dimension=0, tiled=True
     )
-    partial_peak = regroup_peaks(
-        lax.all_to_all(summed, "freq", split_axis=3, concat_axis=1, tiled=True)
-    )
+    partial_peak = regroup_peaks(sent_to_each(summed, "freq", 3, 1))
     whole_peak = lax.pmax(partial_peak, "freq")
     columns = FG // freq_count
     flaw_peak = lax.dynamic_slice_in_dim(whole_peak, lax.axis_index("freq") * columns, columns, 1)

time: 131 us -> 126 us (0.962)
  waiting for transfers between devices: 49.1 us -> 30 us
  blocking collectives: 19.5 us -> 27.7 us
  starting transfers between devices: 5.81 us -> 13.2 us
  other arithmetic: 20.2 us -> 18.2 us
    all_to_all x1 -> x0, waiting for transfers between devices: 26.2 us -> none  [body(): lax.all_to_all(summed, 'freq', split_axis=3, concat_axis=1, tiled=True)]
    ppermute x0 -> x7, starting transfers between devices: none -> 13.1 us  [sent_to_each(): lax.ppermute(sent, axis, [(i, (i + step) % count) for i in range(count)])]
    pmax x1, blocking collectives: 19.5 us -> 27.7 us  [body(): whole_peak = lax.pmax(partial_peak, 'freq')]
    ppermute x0 -> x7, waiting for transfers between devices: none -> 7.18 us  [sent_to_each(): lax.ppermute(sent, axis, [(i, (i + step) % count) for i in range(count)])]
    all_to_all x1 -> x0, starting transfers between devices: 5.78 us -> none  [body(): lax.all_to_all(summed, 'freq', split_axis=3, concat_axis=1, tiled=True)]
    reduce_scatter x1 -> x0, local copies, waits for them, and re-layouts: 1.65 us -> none  [body(): lax.psum_scatter(rounded_term.astype(jnp.bfloat16), 'elem', scatter_dimen...]
    unnamed x9 -> x28, local copies, waits for them, and re-layouts: 6.63 us -> 7.59 us
  transfers between devices with their start and end apart: 2 -> 8, of which waited for: 2 -> 3; matrix products, arithmetic and copies ran while one was open for 0% -> 1% of each run, Pallas kernels for 0% -> 0%
where the time goes in v1:
time: 126 us; the launch traced here: 125 us
  waiting for transfers between devices  30 us (24%)
  blocking collectives  27.7 us (22%)
  local copies, waits for them, and re-layouts  18.3 us (15%)
  other arithmetic  18.2 us (14%)
  between operations  14.4 us (11%)
  starting transfers between devices  13.2 us (10%)
  matrix products  3.2 us (3%)
    pmax x1, blocking collectives, body(): whole_peak = lax.pmax(partial_peak, 'freq')  27.7 us
    unnamed x2, waiting for transfers between devices  22.9 us
    ppermute x7, starting transfers between devices, sent_to_each(): lax.ppermute(sent, axis, [(i, (i + step) % count) for i in range(count)])  13.1 us
    another operation x1, other arithmetic  7.81 us
    unnamed x28, local copies, waits for them, and re-layouts  7.59 us
    ppermute x7, waiting for transfers between devices, sent_to_each(): lax.ppermute(sent, axis, [(i, (i + step) % count) for i in range(count)])  7.18 us
    gather x2, local copies, waits for them, and re-layouts, body(): jnp.take(beam_field, flaw_cells, axis=3)  5.75 us
  transfers between devices with their start and end apart: 8, of which 3 were waited for; matrix products, arithmetic and copies ran while one was open for 1% of the time, Pallas kernels for 0%

profile of v1, /device:TPU:0, one launch (start us, length us, event | category | flops | bytes accessed | tf_op | source)
XLA Modules:
  0.0 125.2 jit_solution(14663995993420371712)
XLA Ops:
  7.2 0.0 copy-start
  7.2 0.0 all-reduce.3.cloned.1.call-start
  7.2 0.7 compare_select_fusion
  7.9 0.7 and_bitcast_fusion
  8.6 3.5 %copy.42 = bf16[16,2,128,256]{2,0,3,1:T(8,128)(2,1)S(1)} copy(bf16[16,2,128,256]{3,2,1,0:T(8,128)(2,1)} %param.14) | data formatting | bytes 4194304 | tf_op args[4]
  12.1 0.1 mul.298
  12.2 0.1 add.299
  12.3 0.1 add.309
  12.4 0.1 add.302
  12.5 2.3 %gather_fusion.2 = bf16[256,16,2,128]{3,1,2,0:T(8,128)(2,1)} fusion(bf16[16,2,128,256]{2,0,3,1:T(8,128)(2,1)S(1)} %copy.42, s32[1024]{0:T(1024)S(1)} %get-tuple-element.169), kind=kCustom, calls=%fused_computation.2 | custom fusion | bytes 4195328 | tf_op jit(solution)/shard_map/jit(_take)/gather | solution.py:140
  14.8 3.5 %copy.44 = bf16[16,2,128,2,128]{4,2,0,3,1:T(8,128)(2,1)S(1)} copy(bf16[16,2,128,2,128]{2,0,1,4,3:T(8,128)(2,1)} %bitcast.123) | data formatting | bytes 4194304 | tf_op jit(solution)/shard_map/jit(_take)/gather | solution.py:140
  18.2 0.2 broadcast_select_fusion.1
  18.5 0.1 slice_bitcast_fusion
  18.6 0.0 copy-start.3
  18.6 0.1 fusion.45
  18.8 0.5 copy-done.3
  19.3 0.5 compare_and_fusion
  19.8 0.1 add.300
  19.9 0.8 gather_fusion
  20.6 1.4 %broadcast_select_fusion.3 = f32[128,256]{1,0:T(8,128)} fusion(f32[128,256]{1,0:T(8,128)S(1)} %gather_fusion, pred[128]{0:T(512)(128)(4,1)} %compare_and_fusion), kind=kLoop, calls=%fused_computation.81 | loop fusion | flops 32768 | bytes 262272 | tf_op jit(solution)/shard_map/jit(_take)/select_n | solution.py:138
  22.0 1.0 copy.41
  23.0 0.5 compare_and_fusion.1
  23.5 1.3 %gather_fusion.1 = f32[256,128]{1,0:T(8,128)} fusion(f32[128,256]{0,1:T(8,128)S(1)} %copy.41, s32[1024]{0:T(1024)S(1)} %get-tuple-element.170), kind=kCustom, calls=%fused_computation.1 | custom fusion | bytes 263168 | tf_op jit(solution)/shard_map/jit(_take)/gather | solution.py:138
  24.9 1.0 broadcast_select_fusion.2
  25.9 7.8 %fusion.30 = (bf16[16,2,128,128]{3,2,0,1:T(8,128)(2,1)S(1)}, bf16[16,2,128,128]{3,2,0,1:T(8,128)(2,1)S(1)}) fusion(f32[2,128,128]{2,1,0:T(8,128)S(1)} %broadcast_select_fusion.2, f32[16]{0:T(128)S(1)} %convert_multiply_fusion), kind=kLoop, calls=%fused_computation.50 | loop fusion | flops 2097152 | bytes 2228288 | tf_op jit(solution)/shard_map/convert.4
  33.7 0.7 broadcast_multiply_fusion.1
  34.4 0.1 fusion.39
  34.6 1.4 %fusion.22 = f32[2,16,128,256]{3,2,1,0:T(8,128)S(1)} fusion(bf16[16,128,2,128]{3,1,0,2:T(8,128)(2,1)S(1)} %get-tuple-element.153, bf16[16,128,2,128]{3,1,0,2:T(8,128)(2,1)S(1)} %fusion.45, bf16[16,128,2,128]{3,1,0,2:T(8,128)(2,1)S(1)} %get-tuple-element.152, bf16[16,2,128,128]{3,2,0,1:T(8,128)(2,1)S(1)} %get-tuple-element.163, ...), kind=kOutput, calls=%fused_computation.40 | convolution fusion | flops 557842432 | bytes 9437184 | tf_op jit(solution)/shard_map/wgre,wegf->gwrf/dot_general | solution.py:146
  36.0 0.6 fusion.36
  36.6 1.5 %pad_maximum_fusion.1 = bf16[2,16,2,128,128]{4,3,1,0,2:T(8,128)(2,1)} fusion(bf16[2,16,1,128,128]{4,3,1,0,2:T(8,128)(2,1)S(1)} %get-tuple-element.151, bf16[2,16,1,128,128]{4,3,1,0,2:T(8,128)(2,1)S(1)} %get-tuple-element.150), kind=kLoop, calls=%fused_computation.56 | loop fusion | flops 1048576 | bytes 4194304 | tf_op jit(solution)/shard_map/stack | solution.py:65
  38.1 0.0 all-reduce.3.cloned.1.call-update
  38.2 0.5 copy-done.4
  38.8 0.6 dynamic-slice.32
  39.4 22.8 %all-reduce.3.cloned.1.call-done = bf16[2,16,2,128,128]{4,3,1,0,2:T(8,128)(2,1)} async-done(((bf16[2,16,2,128,128]{4,3,1,0,2:T(8,128)(2,1)}), bf16[2,16,2,128,128]{4,3,1,0,2:T(8,128)(2,1)}) %all-reduce.3.cloned.1.call-update) | async-done | bytes 2097168
  62.2 1.9 %constant_dynamic-slice_fusion.9 = bf16[1,16,2,128,128]{4,3,1,0,2:T(8,128)(2,1)S(1)} fusion(bf16[2,16,2,128,128]{4,3,1,0,2:T(8,128)(2,1)} %all-reduce.3.cloned.1.call-done, u32[]{:T(128)} %bitcast.50), kind=kLoop, calls=%fused_computation.114 | loop fusion | bytes 2097156
  64.2 0.3 constant_dynamic-slice_fusion.1
  64.5 1.8 %collective-permute-start = (bf16[1,16,2,16,128]{4,3,2,1,0:T(8,128)(2,1)S(1)}, bf16[1,16,2,16,128]{4,3,2,1,0:T(8,128)(2,1)S(1)}, u32[]{:S(2)}, u32[]{:S(2)}) collective-permute-start(bf16[1,16,2,16,128]{4,3,2,1,0:T(8,128)(2,1)S(1)} %bitcast.133), channel_id=1, source_target_pairs={{0,2},{2,4},{4,6},{6,8},{8,10},{10,12},{12,14},{14,0},{1,3},{3,5},... | collective-permute-start | bytes 393224 | tf_op jit(solution)/shard_map/ppermute | solution.py:34
  66.3 1.5 %collective-permute-start.1 = (bf16[1,16,2,16,128]{4,3,2,1,0:T(8,128)(2,1)S(1)}, bf16[1,16,2,16,128]{4,3,2,1,0:T(8,128)(2,1)S(1)}, u32[]{:S(2)}, u32[]{:S(2)}) collective-permute-start(bf16[1,16,2,16,128]{4,3,2,1,0:T(8,128)(2,1)S(1)} %bitcast.132), channel_id=1, source_target_pairs={{0,4},{2,6},{4,8},{6,10},{8,12},{10,14},{12,0},{14,2},{1,5},{3,7},... | collective-permute-start | bytes 393224 | tf_op jit(solution)/shard_map/ppermute | solution.py:34
  67.8 2.5 %collective-permute-start.2 = (bf16[1,16,2,16,128]{4,3,2,1,0:T(8,128)(2,1)S(1)}, bf16[1,16,2,16,128]{4,3,2,1,0:T(8,128)(2,1)S(1)}, u32[]{:S(2)}, u32[]{:S(2)}) collective-permute-start(bf16[1,16,2,16,128]{4,3,2,1,0:T(8,128)(2,1)S(1)} %bitcast.131), channel_id=1, source_target_pairs={{0,6},{2,8},{4,10},{6,12},{8,14},{10,0},{12,2},{14,4},{1,7},{3,9},... | collective-permute-start | bytes 393224 | tf_op jit(solution)/shard_map/ppermute | solution.py:34
  70.3 1.5 %collective-permute-start.3 = (bf16[1,16,2,16,128]{4,3,2,1,0:T(8,128)(2,1)S(1)}, bf16[1,16,2,16,128]{4,3,2,1,0:T(8,128)(2,1)S(1)}, u32[]{:S(2)}, u32[]{:S(2)}) collective-permute-start(bf16[1,16,2,16,128]{4,3,2,1,0:T(8,128)(2,1)S(1)} %bitcast.130), channel_id=1, source_target_pairs={{0,8},{2,10},{4,12},{6,14},{8,0},{10,2},{12,4},{14,6},{1,9},{3,11}... | collective-permute-start | bytes 393224 | tf_op jit(solution)/shard_map/ppermute | solution.py:34
  71.8 2.5 %collective-permute-start.4 = (bf16[1,16,2,16,128]{4,3,2,1,0:T(8,128)(2,1)S(1)}, bf16[1,16,2,16,128]{4,3,2,1,0:T(8,128)(2,1)S(1)}, u32[]{:S(2)}, u32[]{:S(2)}) collective-permute-start(bf16[1,16,2,16,128]{4,3,2,1,0:T(8,128)(2,1)S(1)} %bitcast.129), channel_id=1, source_target_pairs={{0,10},{2,12},{4,14},{6,0},{8,2},{10,4},{12,6},{14,8},{1,11},{3,13... | collective-permute-start | bytes 393224 | tf_op jit(solution)/shard_map/ppermute | solution.py:34
  74.3 0.0 collective-permute-done
  74.3 1.5 %collective-permute-start.5 = (bf16[1,16,2,16,128]{4,3,2,1,0:T(8,128)(2,1)S(1)}, bf16[1,16,2,16,128]{4,3,2,1,0:T(8,128)(2,1)S(1)}, u32[]{:S(2)}, u32[]{:S(2)}) collective-permute-start(bf16[1,16,2,16,128]{4,3,2,1,0:T(8,128)(2,1)S(1)} %bitcast.128), channel_id=1, source_target_pairs={{0,12},{2,14},{4,0},{6,2},{8,4},{10,6},{12,8},{14,10},{1,13},{3,15... | collective-permute-start | bytes 393224 | tf_op jit(solution)/shard_map/ppermute | solution.py:34
  75.8 0.0 collective-permute-done.1
  75.8 1.9 %collective-permute-start.6 = (bf16[1,16,2,16,128]{4,3,2,1,0:T(8,128)(2,1)S(1)}, bf16[1,16,2,16,128]{4,3,2,1,0:T(8,128)(2,1)S(1)}, u32[]{:S(2)}, u32[]{:S(2)}) collective-permute-start(bf16[1,16,2,16,128]{4,3,2,1,0:T(8,128)(2,1)S(1)} %bitcast.127), channel_id=1, source_target_pairs={{0,14},{2,0},{4,2},{6,4},{8,6},{10,8},{12,10},{14,12},{1,15},{3,1}... | collective-permute-start | bytes 393224 | tf_op jit(solution)/shard_map/ppermute | solution.py:34
  77.8 6.6 %collective-permute-done.2 = bf16[1,16,2,16,128]{4,3,2,1,0:T(8,128)(2,1)S(1)} collective-permute-done((bf16[1,16,2,16,128]{4,3,2,1,0:T(8,128)(2,1)S(1)}, bf16[1,16,2,16,128]{4,3,2,1,0:T(8,128)(2,1)S(1)}, u32[]{:S(2)}, u32[]{:S(2)}) %collective-permute-start.2) | collective-permute-done | bytes 131104 | tf_op jit(solution)/shard_map/ppermute | solution.py:34
  84.3 0.6 collective-permute-done.3
  85.0 0.0 collective-permute-done.5
  85.0 0.0 collective-permute-done.6
  85.1 0.7 gather_fusion.3
  85.8 0.3 reshape_reshape_transpose.3
  86.1 0.4 copy.53
  86.5 0.0 copy-start.1
  86.5 3.5 %while.16 = (s32[]{:T(128)}, f32[1,128]{1,0:T(1,128)S(1)}, bf16[1,128,2,2048]{3,1,2,0:T(8,128)(2,1)S(1)}, s32[]{:T(128)}, s32[]{:T(128)}, /*index=5*/s32[]{:T(128)}) while((s32[]{:T(128)}, f32[1,128]{1,0:T(1,128)S(1)}, bf16[1,128,2,2048]{3,1,2,0:T(8,128)(2,1)S(1)}, s32[]{:T(128)}, s32[]{:T(128)}, /*index=5*/s32[]{:T(128)}) %tuple.69), condition=%wide.region_4.5_spmd.clone, body=%wide.region_1.4_spmd.clone.sunk | while | flops 539607296 | bytes 12078183 | solution.py:105
  86.5 0.3 fusion.58
  86.9 0.4 convolution_bitcast_fusion.3
  87.4 0.5 fusion.60
  87.8 0.4 fusion.61
  88.3 0.3 fusion.58
  88.7 0.4 convolution_bitcast_fusion.3
  89.1 0.5 fusion.60
  89.6 0.4 fusion.61
  90.0 27.7 %pmax.7 = f32[1,128]{1,0:T(1,128)S(1)} all-reduce(f32[1,128]{1,0:T(1,128)S(1)} %get-tuple-element.113), channel_id=1, replica_groups=mesh['batch'=2,'freq'=8,'elem'=2] {'freq'}, use_global_device_ids=true, to_apply=%region_5.6 | all-reduce | flops 128 | bytes 1024 | tf_op jit(solution)/shard_map/pmax | solution.py:155
  117.8 0.6 add_divide_fusion
  (41 shorter events, 0.4 us)
Async XLA Ops:
  7.2 12.7 %copy-start = (f32[256,256]{1,0:T(8,128)S(1)}, f32[256,256]{1,0:T(8,128)}, u32[]{:S(2)}) copy-start(f32[256,256]{1,0:T(8,128)} %param.13) | copy-start | bytes 786436
  7.2 55.0 %all-reduce.3.cloned.1.call-start = ((), (), s32[]{:S(2)}) async-start(), calls=%async_computation | async-start | bytes 4194304
  8.6 3.5 %copy-start.2 = (s32[8]{0:T(128)S(1)}, s32[8]{0:T(128)}, u32[]{:S(2)}) copy-start(s32[8]{0:T(128)} %param.11) | copy-start | bytes 100
  18.6 0.7 copy-start.3
  38.1 0.7 copy-start.4
  64.5 9.8 %collective-permute-start = (bf16[1,16,2,16,128]{4,3,2,1,0:T(8,128)(2,1)S(1)}, bf16[1,16,2,16,128]{4,3,2,1,0:T(8,128)(2,1)S(1)}, u32[]{:S(2)}, u32[]{:S(2)}) collective-permute-start(bf16[1,16,2,16,128]{4,3,2,1,0:T(8,128)(2,1)S(1)} %bitcast.133), channel_id=1, source_target_pairs={{0,2},{2,4},{4,6},{6,8},{8,10},{10,12},{12,14},{14,0},{1,3},{3,5},... | collective-permute-start | bytes 393224 | tf_op jit(solution)/shard_map/ppermute | solution.py:34
  66.3 9.6 %collective-permute-start.1 = (bf16[1,16,2,16,128]{4,3,2,1,0:T(8,128)(2,1)S(1)}, bf16[1,16,2,16,128]{4,3,2,1,0:T(8,128)(2,1)S(1)}, u32[]{:S(2)}, u32[]{:S(2)}) collective-permute-start(bf16[1,16,2,16,128]{4,3,2,1,0:T(8,128)(2,1)S(1)} %bitcast.132), channel_id=1, source_target_pairs={{0,4},{2,6},{4,8},{6,10},{8,12},{10,14},{12,0},{14,2},{1,5},{3,7},... | collective-permute-start | bytes 393224 | tf_op jit(solution)/shard_map/ppermute | solution.py:34
  67.8 16.5 %collective-permute-start.2 = (bf16[1,16,2,16,128]{4,3,2,1,0:T(8,128)(2,1)S(1)}, bf16[1,16,2,16,128]{4,3,2,1,0:T(8,128)(2,1)S(1)}, u32[]{:S(2)}, u32[]{:S(2)}) collective-permute-start(bf16[1,16,2,16,128]{4,3,2,1,0:T(8,128)(2,1)S(1)} %bitcast.131), channel_id=1, source_target_pairs={{0,6},{2,8},{4,10},{6,12},{8,14},{10,0},{12,2},{14,4},{1,7},{3,9},... | collective-permute-start | bytes 393224 | tf_op jit(solution)/shard_map/ppermute | solution.py:34
  70.3 14.7 %collective-permute-start.3 = (bf16[1,16,2,16,128]{4,3,2,1,0:T(8,128)(2,1)S(1)}, bf16[1,16,2,16,128]{4,3,2,1,0:T(8,128)(2,1)S(1)}, u32[]{:S(2)}, u32[]{:S(2)}) collective-permute-start(bf16[1,16,2,16,128]{4,3,2,1,0:T(8,128)(2,1)S(1)} %bitcast.130), channel_id=1, source_target_pairs={{0,8},{2,10},{4,12},{6,14},{8,0},{10,2},{12,4},{14,6},{1,9},{3,11}... | collective-permute-start | bytes 393224 | tf_op jit(solution)/shard_map/ppermute | solution.py:34
  71.8 13.2 %collective-permute-start.4 = (bf16[1,16,2,16,128]{4,3,2,1,0:T(8,128)(2,1)S(1)}, bf16[1,16,2,16,128]{4,3,2,1,0:T(8,128)(2,1)S(1)}, u32[]{:S(2)}, u32[]{:S(2)}) collective-permute-start(bf16[1,16,2,16,128]{4,3,2,1,0:T(8,128)(2,1)S(1)} %bitcast.129), channel_id=1, source_target_pairs={{0,10},{2,12},{4,14},{6,0},{8,2},{10,4},{12,6},{14,8},{1,11},{3,13... | collective-permute-start | bytes 393224 | tf_op jit(solution)/shard_map/ppermute | solution.py:34
  74.3 10.7 %collective-permute-start.5 = (bf16[1,16,2,16,128]{4,3,2,1,0:T(8,128)(2,1)S(1)}, bf16[1,16,2,16,128]{4,3,2,1,0:T(8,128)(2,1)S(1)}, u32[]{:S(2)}, u32[]{:S(2)}) collective-permute-start(bf16[1,16,2,16,128]{4,3,2,1,0:T(8,128)(2,1)S(1)} %bitcast.128), channel_id=1, source_target_pairs={{0,12},{2,14},{4,0},{6,2},{8,4},{10,6},{12,8},{14,10},{1,13},{3,15... | collective-permute-start | bytes 393224 | tf_op jit(solution)/shard_map/ppermute | solution.py:34
  75.8 9.2 %collective-permute-start.6 = (bf16[1,16,2,16,128]{4,3,2,1,0:T(8,128)(2,1)S(1)}, bf16[1,16,2,16,128]{4,3,2,1,0:T(8,128)(2,1)S(1)}, u32[]{:S(2)}, u32[]{:S(2)}) collective-permute-start(bf16[1,16,2,16,128]{4,3,2,1,0:T(8,128)(2,1)S(1)} %bitcast.127), channel_id=1, source_target_pairs={{0,14},{2,0},{4,2},{6,4},{8,6},{10,8},{12,10},{14,12},{1,15},{3,1}... | collective-permute-start | bytes 393224 | tf_op jit(solution)/shard_map/ppermute | solution.py:34
  86.5 31.3 %copy-start.1 = (f32[1,16]{1,0:T(1,128)S(1)}, f32[1,16]{1,0:T(1,128)}, u32[]{:S(2)}) copy-start(f32[1,16]{1,0:T(1,128)} %param.17) | copy-start | bytes 196
Sparse Core Ops, SparseCore 0:
  38.3 23.9 all-reduce.2
